TPU v7x, 128 devices: a whole 4x4x4 slice. The times are simulated.
128 devices in a mesh: lat: 8 (over x, core), lon: 16 (over y, z).
Axes of the slice: x: 4, y: 4, z: 4, core: 2. Of those that a mesh axis runs over, the one named last changes fastest.
Arguments:
- vorticity: float32 [16, 2, 256, 8192], P(None, None, 'lat', 'lon'), may hold values from -6 to 6
- legendre: bfloat16 [2048, 2048, 256], P(('lat', 'lon')), may hold values from -0.25 to 0.25
- wave_order: int32 [2048], replicated, may hold values from 0 to 2047, each once
Outputs:
- spectral: float32 [2048, 2, 16, 2048], P(('lat', 'lon'))
Inputs may be any that keep to these rules, and one draw needn't show every extreme that they name: wave_order is a permutation: every wavenumber below 2048 is held by exactly one slot.
All inputs are finite; a program needn't handle non-finite values.
Results may differ from a plain program's by a relative error of at most 0.0029.
Values may be sent and summed in bfloat16 or wider, within the bound.
A program may use at most 128 MiB of HBM per device.

v0:
```python
import math

import jax
import jax.numpy as jnp
from jax import lax
from jax.sharding import PartitionSpec as P

MW = 2048


def angle_table(first_index, second_index, period):
    product = first_index[:, None] * second_index[None, :] % period
    return 2.0 * math.pi / period * product.astype(jnp.float32)


def fourier_rows(received):
    levels, hemis, items, circle = received.shape
    second_len = circle // 64
    kept_second = MW // 64
    flat_rows = received.reshape(levels * hemis * items, 64, second_len)
    index_first = jnp.arange(64, dtype=jnp.int32)
    index_second = jnp.arange(second_len, dtype=jnp.int32)
    index_kept = jnp.arange(kept_second, dtype=jnp.int32)
    angle_first = angle_table(index_first, index_first, 64)
    cos_first = jnp.cos(angle_first)
    sin_first = jnp.sin(angle_first)
    high = lax.Precision.HIGHEST
    first_real = jnp.einsum("rab,ak->rkb", flat_rows, cos_first, precision=high)
    first_imag = -jnp.einsum("rab,ak->rkb", flat_rows, sin_first, precision=high)
    angle_twist = (
        2.0
        * math.pi
        / circle
        * (index_first[:, None] * index_second[None, :] % circle).astype(jnp.float32)
    )
    twist_cos = jnp.cos(angle_twist)
    twist_sin = jnp.sin(angle_twist)
    middle_real = first_real * twist_cos + first_imag * twist_sin
    middle_imag = first_imag * twist_cos - first_real * twist_sin
    angle_second = angle_table(index_second, index_kept, second_len)
    cos_second = jnp.cos(angle_second)
    sin_second = jnp.sin(angle_second)
    final_real = jnp.einsum("rkb,bq->rqk", middle_real, cos_second, precision=high) + jnp.einsum(
        "rkb,bq->rqk", middle_imag, sin_second, precision=high
    )
    final_imag = jnp.einsum("rkb,bq->rqk", middle_imag, cos_second, precision=high) - jnp.einsum(
        "rkb,bq->rqk", middle_real, sin_second, precision=high
    )
    stacked = jnp.stack([final_real, final_imag], axis=1) * (1.0 / math.sqrt(circle))
    return stacked.reshape(levels, hemis, items, 2, MW).astype(jnp.bfloat16)


def combine_parts(product, parity, limit_rows, degree_cols, levels):
    count = product.shape[0]
    product = product.reshape(count, 2, 2, levels, product.shape[-1])
    combined = product[:, 0] + parity * product[:, 1]
    keep_mask = degree_cols[None, :] < limit_rows[:, None]
    return jnp.where(keep_mask[:, None, None, :], combined, jnp.zeros_like(combined))


def on_device(vorticity, legendre, wave_order):
    fourier = fourier_rows(
        lax.all_to_all(vorticity, "lon", split_axis=0, concat_axis=3, tiled=True)
    )
    chosen = jnp.take(fourier, wave_order, axis=4)
    packed = chosen[None, None]
    moved = lax.all_to_all(packed, ("lat", "lon"), split_axis=6, concat_axis=0, tiled=True)
    moved = moved.reshape((lax.axis_size("lat"), lax.axis_size("lon")) + moved.shape[2:])
    per_slot = jnp.transpose(moved, (6, 0, 4, 3, 5, 1, 2))
    slot_count = per_slot.shape[0]
    lat_total = per_slot.shape[1] * per_slot.shape[2]
    column_count = per_slot.shape[3] * per_slot.shape[4] * per_slot.shape[5] * per_slot.shape[6]
    levels = per_slot.shape[5] * per_slot.shape[6]
    per_slot = per_slot.reshape(slot_count, lat_total, column_count)
    wave_total = wave_order.shape[0]
    degree_count = legendre.shape[1]
    first_slot = lax.axis_index(("lat", "lon")) * slot_count
    local_waves = lax.dynamic_slice_in_dim(wave_order, first_slot, slot_count)
    limits = wave_total - local_waves
    degree_cols = jnp.arange(degree_count, dtype=jnp.int32)
    parity = (1 - 2 * (degree_cols % 2)).astype(jnp.float32)
    product = jnp.einsum("skj,sjq->sqk", legendre, per_slot, preferred_element_type=jnp.float32)
    return combine_parts(product, parity, limits, degree_cols, levels)


def solution(mesh):
    placed = (P(None, None, "lat", "lon"), P(("lat", "lon"), None, None), P())
    return jax.shard_map(
        on_device,
        mesh=mesh,
        in_specs=placed,
        out_specs=P(("lat", "lon"), None, None, None),
        check_vma=False,
    )
```

profile of v0, /device:TPU:1, one launch (start us, length us, event | category | flops | bytes accessed | tf_op | source)
XLA Modules:
  0.0 155.7 jit_solution(4832311974008011177)
XLA Ops:
  0.0 8.7 %all-to-all-start = ((f32[16,2,32,512]{3,2,1,0:T(8,128)}), f32[16,2,32,512]{3,2,1,0:T(8,128)S(1)}, u32[]{:S(2)}, u32[]{:S(2)}) async-start(f32[16,2,32,512]{3,2,1,0:T(8,128)} %param.3), calls=%async_computation | async-start | bytes 4194304 | tf_op jit(solution)/shard_map/all_to_all | solution.py:63
  8.7 0.1 fusion.51
  8.9 0.0 copy-done.2
  8.9 28.0 %all-to-all-done = f32[16,2,32,512]{3,2,1,0:T(8,128)S(1)} async-done(((f32[16,2,32,512]{3,2,1,0:T(8,128)}), f32[16,2,32,512]{3,2,1,0:T(8,128)S(1)}, u32[]{:S(2)}, u32[]{:S(2)}) %all-to-all-start) | async-done | bytes 2097184 | tf_op jit(solution)/shard_map/all_to_all | solution.py:63
  36.9 2.5 %copy.26 = f32[1,2,32,16,512]{4,3,2,1,0:T(8,128)} copy(f32[1,2,32,16,512]{4,2,1,3,0:T(8,128)S(1)} %bitcast.95) | data formatting | bytes 4194304 | tf_op jit(solution)/shard_map/all_to_all | solution.py:63
  39.4 2.6 %reshape.137 = f32[64,64,128]{2,1,0:T(8,128)} reshape(f32[1,2,32,16,512]{4,3,2,1,0:T(8,128)} %copy.26) | data formatting | bytes 4194304 | tf_op jit(solution)/shard_map/reshape | solution.py:20
  42.1 3.7 %fusion.32 = f32[64,64,128]{2,0,1:T(8,128)S(1)} fusion(f32[64,64,128]{2,1,0:T(8,128)} %reshape.137), kind=kOutput, calls=%fused_computation.38 | convolution fusion | flops 402710528 | bytes 4194304 | tf_op jit(solution)/shard_map/rab,ak->rkb/dot_general | solution.py:29
  45.8 2.1 %fusion.34 = f32[64,64,128]{2,0,1:T(8,128)S(1)} fusion(f32[64,64,128]{2,1,0:T(8,128)S(1)} %copy-done.1), kind=kOutput, calls=%fused_computation.40 | convolution fusion | flops 402710528 | bytes 4194304 | tf_op jit(solution)/shard_map/rab,ak->rkb/dot_general | solution.py:28
  47.9 0.0 copy-start
  48.0 5.9 %fusion.3 = f32[32,64,64]{2,0,1:T(8,128)S(1)} fusion(f32[64,64,128]{2,0,1:T(8,128)S(1)} %fusion.34, f32[64,64,128]{2,0,1:T(8,128)S(1)} %fusion.32, f32[64,128]{1,0:T(8,128)S(1)} %get-tuple-element.5, f32[64,128]{1,0:T(8,128)S(1)} %get-tuple-element.6), kind=kOutput, calls=%fused_computation.7 | convolution fusion | flops 203481088 | bytes 4784128 | tf_op jit(solution)/shard_map/rkb,bq->rqk/dot_general | solution.py:46
  53.8 6.8 %fusion.5 = f32[32,64,64]{2,0,1:T(8,128)} fusion(f32[64,64,128]{2,0,1:T(8,128)S(1)} %fusion.34, f32[64,64,128]{2,0,1:T(8,128)S(1)} %fusion.32, f32[64,128]{1,0:T(8,128)S(1)} %get-tuple-element.5, f32[64,128]{1,0:T(8,128)S(1)} %get-tuple-element.6), kind=kOutput, calls=%fused_computation.9 | convolution fusion | flops 203481088 | bytes 4784128 | tf_op jit(solution)/shard_map/rkb,bq->rqk/dot_general | solution.py:43
  60.6 0.0 copy-done
  60.6 6.0 %fusion.21 = f32[64,32,64]{2,1,0:T(8,128)S(1)} fusion(f32[32,64,64]{2,0,1:T(8,128)S(1)} %fusion.3, f32[64,64,128]{2,0,1:T(8,128)S(1)} %fusion.34, f32[64,64,128]{2,0,1:T(8,128)S(1)} %fusion.32, f32[64,128]{1,0:T(8,128)S(1)} %get-tuple-element.5, f32[64,128]{1,0:T(8,128)S(1)} %get-tuple-element.6), kind=kOutput, calls=%fused_computation.21 | convolution fusion | flops 203612160 | bytes 5308416 | tf_op jit(solution)/shard_map/rkb,bq->rqk/dot_general | solution.py:46
  66.7 1.2 stack.10
  67.8 7.7 %fusion.15 = f32[64,32,64]{2,1,0:T(8,128)S(1)} fusion(f32[32,64,64]{2,0,1:T(8,128)} %fusion.5, f32[64,64,128]{2,0,1:T(8,128)} %copy-done, f32[64,64,128]{2,0,1:T(8,128)S(1)} %fusion.32, f32[64,128]{1,0:T(8,128)S(1)} %get-tuple-element.5, f32[64,128]{1,0:T(8,128)S(1)} %get-tuple-element.6), kind=kOutput, calls=%fused_computation.19 | convolution fusion | flops 203612160 | bytes 5308416 | tf_op jit(solution)/shard_map/rkb,bq->rqk/dot_general | solution.py:43
  75.5 0.4 stack.9
  75.9 1.1 fusion.25
  77.0 1.5 copy.29
  78.5 16.9 %gather_fusion = bf16[2048,2,32,2]{2,3,1,0:T(2,128)(2,1)} fusion(bf16[2,32,2,2048]{1,2,3,0:T(2,128)(2,1)S(1)} %copy.29, s32[2048]{0:T(1024)S(1)} %fusion.70), kind=kCustom, calls=%fused_computation | custom fusion | bytes 1056768 | tf_op jit(solution)/shard_map/jit(_take)/gather | solution.py:65
  95.4 9.2 %fusion.95 = bf16[2048,1,1,1,2,2,32]{6,5,4,3,2,1,0:T(2,128)(2,1)S(1)} fusion(bf16[2048,2,32,2]{2,3,1,0:T(2,128)(2,1)} %gather_fusion, pred[2048]{0:T(1024)(128)(4,1)S(1)} %compare_and_fusion), kind=kLoop, calls=%fused_computation.103 | loop fusion | flops 262144 | bytes 1050624
  104.6 2.8 %reshape.157 = bf16[128,2,1024]{2,1,0:T(2,128)(2,1)} reshape(bf16[2048,1,1,1,2,2,32]{6,5,4,3,2,1,0:T(2,128)(2,1)S(1)} %fusion.95) | data formatting | bytes 1048576
  107.4 8.7 %all-to-all-start.1 = ((bf16[128,2,1024]{2,1,0:T(2,128)(2,1)}), bf16[128,2,1024]{2,1,0:T(2,128)(2,1)S(1)}, u32[]{:S(2)}, u32[]{:S(2)}) async-start(bf16[128,2,1024]{2,1,0:T(2,128)(2,1)} %reshape.157), calls=%async_computation.1 | async-start | bytes 1048576 | tf_op jit(solution)/shard_map/all_to_all | solution.py:67
  116.1 0.1 dynamic-slice_subtract_fusion
  116.2 0.1 iota_compare_fusion
  116.3 13.7 %all-to-all-done.1 = bf16[128,2,1024]{2,1,0:T(2,128)(2,1)S(1)} async-done(((bf16[128,2,1024]{2,1,0:T(2,128)(2,1)}), bf16[128,2,1024]{2,1,0:T(2,128)(2,1)S(1)}, u32[]{:S(2)}, u32[]{:S(2)}) %all-to-all-start.1) | async-done | bytes 524320 | tf_op jit(solution)/shard_map/all_to_all | solution.py:67
  130.0 1.0 reshape.158
  131.0 0.3 copy.31
  131.3 0.7 copy.32
  131.9 1.4 copy.33
  133.3 1.5 reshape.139
  134.8 14.1 %fusion.96 = f32[16,64,2048]{2,1,0:T(8,128)} fusion(bf16[16,256,64]{1,2,0:T(8,128)(2,1)S(1)} %reshape.139, bf16[16,2048,256]{2,1,0:T(8,128)(2,1)} %param.4), kind=kOutput, calls=%fused_computation.104 | convolution fusion | flops 1073741824 | bytes 25690112 | tf_op jit(solution)/shard_map/skj,sjq->sqk/dot_general | solution.py:82
  148.9 6.8 %fusion.2 = f32[16,2,16,2048]{3,2,1,0:T(8,128)} fusion(f32[16,2,2,16,2048]{4,3,2,1,0:T(8,128)} %bitcast.93, f32[2048]{0:T(1024)S(1)} %fusion.60, pred[16,2048]{1,0:T(8,128)(4,1)S(1)} %iota_compare_fusion), kind=kLoop, calls=%fused_computation.4 | loop fusion | flops 3145728 | bytes 12623872 | tf_op jit(solution)/shard_map/jit(_where)/select_n | solution.py:58
  (6 shorter events, 0.0 us)
Async XLA Ops:
  0.0 8.9 %copy-start.2 = (s32[2048]{0:T(1024)S(1)}, s32[2048]{0:T(1024)}, u32[]{:S(2)}) copy-start(s32[2048]{0:T(1024)} %param.5) | copy-start | bytes 24580
  0.0 36.9 %all-to-all-start = ((f32[16,2,32,512]{3,2,1,0:T(8,128)}), f32[16,2,32,512]{3,2,1,0:T(8,128)S(1)}, u32[]{:S(2)}, u32[]{:S(2)}) async-start(f32[16,2,32,512]{3,2,1,0:T(8,128)} %param.3), calls=%async_computation | async-start | bytes 4194304 | tf_op jit(solution)/shard_map/all_to_all | solution.py:63
  42.1 3.7 %copy-start.1 = (f32[64,64,128]{2,1,0:T(8,128)S(1)}, f32[64,64,128]{2,1,0:T(8,128)}, u32[]{:S(2)}) copy-start(f32[64,64,128]{2,1,0:T(8,128)} %reshape.137) | copy-start | bytes 6291460
  47.9 12.7 %copy-start = (f32[64,64,128]{2,0,1:T(8,128)}, f32[64,64,128]{2,0,1:T(8,128)S(1)}, u32[]{:S(2)}) copy-start(f32[64,64,128]{2,0,1:T(8,128)S(1)} %fusion.34) | copy-start | bytes 6291460
  107.4 22.6 %all-to-all-start.1 = ((bf16[128,2,1024]{2,1,0:T(2,128)(2,1)}), bf16[128,2,1024]{2,1,0:T(2,128)(2,1)S(1)}, u32[]{:S(2)}, u32[]{:S(2)}) async-start(bf16[128,2,1024]{2,1,0:T(2,128)(2,1)} %reshape.157), calls=%async_computation.1 | async-start | bytes 1048576 | tf_op jit(solution)/shard_map/all_to_all | solution.py:67
where the time goes:
time: 156 us
  matrix products  46.4 us (30%)
  waiting for transfers between devices  41.6 us (27%)
  local copies, waits for them, and re-layouts  32.6 us (21%)
  other arithmetic  17.5 us (11%)
  starting transfers between devices  17.4 us (11%)
    all_to_all x1, waiting for transfers between devices, on_device(): lax.all_to_all(vorticity, 'lon', split_axis=0, concat_axis=3, tiled=True)  28 us
    gather x1, local copies, waits for them, and re-layouts, on_device(): chosen = jnp.take(fourier, wave_order, axis=4)  16.9 us
    dot_general x1, matrix products, on_device(): jnp.einsum('skj,sjq->sqk', legendre, per_slot, preferred_element_type=jnp...  14.1 us
    all_to_all x1, waiting for transfers between devices, on_device(): lax.all_to_all(packed, ('lat', 'lon'), split_axis=6, concat_axis=0, tiled...  13.7 us
    unnamed x1, other arithmetic  9.2 us
    all_to_all x1, starting transfers between devices, on_device(): lax.all_to_all(packed, ('lat', 'lon'), split_axis=6, concat_axis=0, tiled...  8.73 us
    all_to_all x1, starting transfers between devices, on_device(): lax.all_to_all(vorticity, 'lon', split_axis=0, concat_axis=3, tiled=True)  8.72 us
    dot_general x1, matrix products, fourier_rows(): jnp.einsum('rkb,bq->rqk', middle_real, cos_second, precision=high)  7.69 us
  transfers between devices with their start and end apart: 2, of which 2 were waited for; matrix products, arithmetic and copies ran while one was open for 0% of the time, Pallas kernels for 0%

commit v1 on v0

v1 whole, which is shorter than its diff:
```python
import functools
import math

import jax
import jax.numpy as jnp
import numpy as np
from jax import lax
from jax.experimental import pallas as pl
from jax.experimental.pallas import tpu as pltpu
from jax.sharding import PartitionSpec as P

NLON = 8192
MW = 2048
BLOCKS = 16
SPAN = NLON // BLOCKS
HALF = MW // BLOCKS
CIRCLES = 64
ROWS = 16
MESH = pl.DeviceIdType.MESH


@functools.cache
def tables():
    n = np.arange(SPAN)
    wave = np.arange(HALF)
    phase = 2.0 * np.pi / (2 * SPAN) * (n[None, :] * (2 * wave[:, None] + 1) % (2 * SPAN))
    basis = np.concatenate([np.cos(phase), np.sin(phase)]) / math.sqrt(NLON)
    high = basis.astype(jnp.bfloat16)
    low = (basis - high.astype(np.float64)).astype(jnp.bfloat16)
    first = np.arange(BLOCKS // 2 + 1) - BLOCKS // 2
    angle = 2.0 * np.pi / NLON * (n[None, :] * first[:, None])
    twiddle = np.zeros((24, SPAN), np.float32)
    twiddle[0:9] = np.cos(angle)
    twiddle[9:18] = -np.sin(angle)
    return np.concatenate([high, low]), twiddle


def real_dft(xs):
    n = len(xs)
    if n == 2:
        return [(xs[0] + xs[1], None), (xs[0] - xs[1], None)]
    evens, odds = real_dft(xs[0::2]), real_dft(xs[1::2])
    out = [None] * (n // 2 + 1)
    for k in range(n // 4 + 1):
        (er, ei), (orr, oi) = evens[k], odds[k]
        if k == 0:
            out[0], out[n // 2] = (er + orr, None), (er - orr, None)
        elif k == n // 4:
            out[k] = (er, -orr)
        else:
            c, s = math.cos(2 * math.pi * k / n), math.sin(2 * math.pi * k / n)
            tr, ti = (c * orr, -s * orr) if oi is None else (c * orr + s * oi, c * oi - s * orr)
            out[k] = (er + tr, ti if ei is None else ei + ti)
            out[n // 2 - k] = (er - tr, ti if ei is None else ti - ei)
    return out


def split(x):
    high = x.astype(jnp.bfloat16)
    return high, (x - high.astype(jnp.float32)).astype(jnp.bfloat16)


NT = (((1,), (1,)), ((), ()))
CHUNKS = 4
CROWS = CIRCLES // CHUNKS


def fourier_kernel(
    lat_n, lon_n, order, v_hbm, basis_hbm, twiddle, out_ref,
    v_in, basis, sent, got, z_high, z_low, fourier, picked, packed,
    load_sem, send_sem, recv_sem, own_sem, out_send, out_recv, out_own,
):
    lat, lon = lax.axis_index("lat"), lax.axis_index("lon")
    v_copy = pltpu.make_async_copy(v_hbm, v_in, load_sem.at[0])
    v_copy.start()
    basis_copy = pltpu.make_async_copy(basis_hbm, basis, load_sem.at[1])
    basis_copy.start()

    barrier = pltpu.get_barrier_semaphore()
    for step in range(1, lon_n):
        peer = lax.rem(lon + step, lon_n)
        pl.semaphore_signal(barrier, inc=1, device_id=(lat, peer), device_id_type=MESH)
    for step in range(1, lat_n):
        peer = lax.rem(lat + step, lat_n)
        pl.semaphore_signal(barrier, inc=1, device_id=(peer, lon), device_id_type=MESH)

    v_copy.wait()

    @pl.loop(0, lon_n)
    def _(level):
        for c in range(CHUNKS):
            h, j = divmod(c * CROWS, 32)
            sent[level, c] = v_in[level, h, j : j + CROWS, :].astype(jnp.bfloat16)

    own = pltpu.make_async_copy(sent.at[lon], got.at[lon], own_sem)
    own.start()
    pl.semaphore_wait(barrier, lon_n - 1 + lat_n - 1)

    def exchange(c, step):
        peer = lax.rem(lon + step, lon_n)
        return pltpu.make_async_remote_copy(
            src_ref=sent.at[peer, c],
            dst_ref=got.at[lon, c],
            send_sem=send_sem.at[c],
            recv_sem=recv_sem.at[c],
            device_id=(lat, peer),
            device_id_type=MESH,
        )

    for c in range(CHUNKS):

        @pl.loop(1, lon_n)
        def _(step):
            exchange(c, step).start()

    basis_copy.wait()
    own.wait()
    for c in range(CHUNKS):
        pltpu.make_async_copy(got.at[pl.ds(1, lon_n - 1), c], got.at[pl.ds(1, lon_n - 1), c], recv_sem.at[c]).wait()

        @pl.loop(0, SPAN // 128)
        def _(part):
            lanes = pl.ds(pl.multiple_of(part * 128, 128), 128)
            blocks = [got[b, c, :, lanes].astype(jnp.float32) for b in range(BLOCKS)]
            for k, (yr, yi) in enumerate(real_dft(blocks)):
                row = k * 2 * CIRCLES + c * CROWS
                if k == BLOCKS // 2:
                    zr, zi = yr, None
                else:
                    tc, ts = twiddle[k : k + 1, lanes], twiddle[k + 9 : k + 10, lanes]
                    if yi is None:
                        zr, zi = yr * tc, yr * ts
                    else:
                        zr, zi = yr * tc - yi * ts, yr * ts + yi * tc
                high, low = split(zr)
                z_high[pl.ds(row, CROWS), lanes] = high
                z_low[pl.ds(row, CROWS), lanes] = low
                row += CIRCLES
                if zi is None:
                    high = low = jnp.zeros((CROWS, 128), jnp.bfloat16)
                else:
                    high, low = split(zi)
                z_high[pl.ds(row, CROWS), lanes] = high
                z_low[pl.ds(row, CROWS), lanes] = low

    lane = lax.broadcasted_iota(jnp.int32, (1, 128), 1)
    sign = jnp.where(lane < CIRCLES, 1.0, -1.0).astype(jnp.float32)
    for k in range(BLOCKS // 2 + 1):
        rows = pl.ds(k * 128, 128)
        by_high = lax.dot_general(basis[...], z_high[rows, :], NT, preferred_element_type=jnp.float32)
        by_low = lax.dot_general(basis[: 2 * HALF, :], z_low[rows, :], NT, preferred_element_type=jnp.float32)
        both = by_high[: 2 * HALF] + by_high[2 * HALF :] + by_low
        cos_part = both[:HALF]
        sin_part = pltpu.roll(both[HALF:], CIRCLES, 1)
        fourier[pl.ds(k, HALF, stride=BLOCKS), :] = cos_part + sign * sin_part
        if 0 < k < BLOCKS // 2:
            fourier[pl.ds(BLOCKS - k, HALF, stride=BLOCKS), :] = sign * cos_part - sin_part

    me = lat * lon_n + lon
    n = lat_n * lon_n

    @pl.loop(0, n)
    def _(step):
        to = lax.rem(me + step, n)
        base = to * ROWS
        for r in range(ROWS):
            picked[pl.ds(step * ROWS + r, 1), :] = fourier[pl.ds(order[base + r], 1), :]
        packed[step] = picked[pl.ds(pl.multiple_of(step * ROWS, ROWS), ROWS), :].astype(jnp.bfloat16)

    pltpu.make_async_copy(packed.at[0], out_ref.at[me], out_own).start()

    @pl.loop(1, n)
    def _(step):
        to = lax.rem(me + step, n)
        pltpu.make_async_remote_copy(
            src_ref=packed.at[step],
            dst_ref=out_ref.at[me],
            send_sem=out_send,
            recv_sem=out_recv,
            device_id=(to // lon_n, lax.rem(to, lon_n)),
            device_id_type=MESH,
        ).start()

    for c in range(CHUNKS):
        pltpu.make_async_copy(sent.at[pl.ds(1, lon_n - 1), c], sent.at[pl.ds(1, lon_n - 1), c], send_sem.at[c]).wait()
    pltpu.make_async_copy(packed.at[0], out_ref.at[me], out_own).wait()
    rest = packed.at[pl.ds(1, n - 1)]
    pltpu.make_async_copy(rest, rest, out_send).wait()
    pltpu.make_async_copy(rest, rest, out_recv).wait()


KB = 256


def legendre_kernel(limits, moved_ref, table, out, table_in, moved, data, result, table_sem, out_sem):
    slots, degrees, lats = table_in.shape
    parts = degrees // KB

    def fetch(s, p):
        at = pl.ds(pl.multiple_of(p * KB, KB), KB)
        return pltpu.make_async_copy(table.at[s, at], table_in.at[s, at], table_sem.at[s])

    @pl.loop(0, slots)
    def _(s):
        for p in range(parts):

            @pl.when(p * KB < limits[s])
            def _():
                fetch(s, p).start()

    @pl.loop(0, 128)
    def _(source):
        moved[pl.ds(pl.multiple_of(source * ROWS, ROWS), ROWS), :] = moved_ref[source].astype(jnp.float32)

    lane = lax.broadcasted_iota(jnp.int32, (16, 128), 1) // 32

    @pl.loop(0, slots)
    def _(s):
        for half in range(2):
            xs = [moved[pl.ds((half * 4 + i) * 256 + s, 16, stride=ROWS), :] for i in range(4)]
            for g in range(4):
                rolled = [x if i == g else pltpu.roll(x, (i - g) % 4 * 32, 1) for i, x in enumerate(xs)]
                joined = jnp.where(lane < 2, jnp.where(lane < 1, rolled[0], rolled[1]), jnp.where(lane < 3, rolled[2], rolled[3]))
                data[s, pl.ds(g * 16, 16), pl.ds(half * 128, 128)] = joined.astype(jnp.bfloat16)

    degree = lax.broadcasted_iota(jnp.int32, (1, KB), 1)
    parity = (1 - 2 * (degree % 2)).astype(jnp.float32)

    @pl.loop(0, slots)
    def _(s):
        for p in range(parts):
            at = pl.ds(p * KB, KB)
            needed = p * KB < limits[s]

            @pl.when(needed)
            def _():
                fetch(s, p).wait()
                sums = lax.dot_general(data[s], table_in[s, at, :], NT, preferred_element_type=jnp.float32)
                keep = degree + p * KB < limits[s]
                for c in range(2):
                    both = sums[c * 32 : c * 32 + 16] + parity * sums[c * 32 + 16 : c * 32 + 32]
                    result[s, c, :, at] = jnp.where(keep, both, 0.0)

            @pl.when(jnp.logical_not(needed))
            def _():
                for c in range(2):
                    result[s, c, :, at] = jnp.zeros((16, KB), jnp.float32)

        pltpu.make_async_copy(result.at[s], out.at[s], out_sem).start()

    pltpu.make_async_copy(result, out, out_sem).wait()


def on_device(vorticity, legendre, wave_order):
    lat_n, lon_n = lax.axis_size("lat"), lax.axis_size("lon")
    n = lat_n * lon_n
    basis, twiddle = tables()
    bf16, f32 = jnp.bfloat16, jnp.float32
    hbm = pl.BlockSpec(memory_space=pl.ANY)
    vmem = pl.BlockSpec(memory_space=pltpu.VMEM)
    smem = pl.BlockSpec(memory_space=pltpu.SMEM)
    dma = pltpu.SemaphoreType.DMA
    moved = pl.pallas_call(
        functools.partial(fourier_kernel, lat_n, lon_n),
        out_shape=jax.ShapeDtypeStruct((n, ROWS, 128), bf16),
        in_specs=[smem, hbm, hbm, vmem],
        out_specs=hbm,
        scratch_shapes=[
            pltpu.VMEM(vorticity.shape, f32),
            pltpu.VMEM(basis.shape, bf16),
            pltpu.VMEM((lon_n, CHUNKS, CROWS, SPAN), bf16),
            pltpu.VMEM((lon_n, CHUNKS, CROWS, SPAN), bf16),
            pltpu.VMEM((9 * 128, SPAN), bf16),
            pltpu.VMEM((9 * 128, SPAN), bf16),
            pltpu.VMEM((MW, 128), f32),
            pltpu.VMEM((MW, 128), f32),
            pltpu.VMEM((n, ROWS, 128), bf16),
            dma((2,)),
            dma((CHUNKS,)),
            dma((CHUNKS,)),
            dma,
            dma,
            dma,
            dma,
        ],
        compiler_params=pltpu.CompilerParams(collective_id=0, has_side_effects=True),
        name="fourier",
    )(wave_order, vorticity, jnp.asarray(basis), jnp.asarray(twiddle))

    first_slot = lax.axis_index(("lat", "lon")) * ROWS
    limits = MW - lax.dynamic_slice_in_dim(wave_order, first_slot, ROWS)
    slots, degrees, lats = legendre.shape
    return pl.pallas_call(
        legendre_kernel,
        out_shape=jax.ShapeDtypeStruct((slots, 2, 16, degrees), f32),
        in_specs=[smem, vmem, hbm],
        out_specs=hbm,
        scratch_shapes=[
            pltpu.VMEM(legendre.shape, bf16),
            pltpu.VMEM((MW, 128), f32),
            pltpu.VMEM((slots, 64, lats), bf16),
            pltpu.VMEM((slots, 2, 16, degrees), f32),
            dma((slots,)),
            dma,
        ],
        name="legendre_sums",
    )(limits, moved, legendre)


def solution(mesh):
    placed = (P(None, None, "lat", "lon"), P(("lat", "lon"), None, None), P())
    return jax.shard_map(
        on_device,
        mesh=mesh,
        in_specs=placed,
        out_specs=P(("lat", "lon"), None, None, None),
        check_vma=False,
    )
```

time: 156 us -> 61.2 us (0.39)
  the two profiles are of different devices: /device:TPU:1 before, /device:TPU:9 now
where the time goes in v1:
time: 61.2 us; the launch traced here: 60.3 us
  Pallas kernels  58.9 us (96%)
  other arithmetic  1.35 us (2%)
    pallas_call x1, Pallas kernels, on_device(): pl.pallas_call(functools.partial(fourier_kernel, lat_n, lon_n), out_shape...  37.8 us
    pallas_call x1, Pallas kernels, on_device(): pl.pallas_call(legendre_kernel, out_shape=jax.ShapeDtypeStruct((slots, 2,...  21.1 us
    sub x1, other arithmetic, on_device(): limits = MW - lax.dynamic_slice_in_dim(wave_order, first_slot, ROWS)  1.35 us

profile of v1, /device:TPU:9, one launch (start us, length us, event | category | flops | bytes accessed | tf_op | source)
XLA Modules:
  0.0 60.3 jit_solution(12058881951373363616)
XLA Ops:
  0.0 1.4 %dynamic-slice_subtract_fusion.limits = s32[16]{0:T(128)} fusion(s32[2048]{0:T(1024)} %order.1, s32[]{:T(128)S(6)} %select_n.3), kind=kLoop, calls=%fused_computation | loop fusion | flops 16 | bytes 132 | tf_op jit(solution)/shard_map/sub | solution.py:291
  1.4 37.8 %fourier.1.moved_ref = bf16[128,16,128]{2,1,0:T(8,128)(2,1)} custom-call(s32[2048]{0:T(1024)} %order.1, f32[16,2,32,512]{3,2,1,0:T(8,128)} %v_hbm.1, bf16[512,512]{1,0:T(8,128)(2,1)} %constant.20.clone.basis_hbm, f32[24,512]{1,0:T(8,128)} %constant.21.clone.twiddle), custom_call_target="tpu_custom_call" | custom-call | tf_op jit(solution)/shard_map/fourier/pallas_call | solution.py:263
  39.2 21.1 %legendre_sums.1 = f32[16,2,16,2048]{3,2,1,0:T(8,128)} custom-call(s32[16]{0:T(128)} %dynamic-slice_subtract_fusion.limits, bf16[128,16,128]{2,1,0:T(8,128)(2,1)} %fourier.1.moved_ref, bf16[16,2048,256]{2,1,0:T(8,128)(2,1)} %table.1), custom_call_target="tpu_custom_call" | custom-call | tf_op jit(solution)/shard_map/legendre_sums/pallas_call | solution.py:293

commit v2 on v1

--- a/solution.py
+++ b/solution.py
@@ -159,27 +159,30 @@
     me = lat * lon_n + lon
     n = lat_n * lon_n
 
-    @pl.loop(0, n)
-    def _(step):
-        to = lax.rem(me + step, n)
-        base = to * ROWS
-        for r in range(ROWS):
-            picked[pl.ds(step * ROWS + r, 1), :] = fourier[pl.ds(order[base + r], 1), :]
-        packed[step] = picked[pl.ds(pl.multiple_of(step * ROWS, ROWS), ROWS), :].astype(jnp.bfloat16)
-
-    pltpu.make_async_copy(packed.at[0], out_ref.at[me], out_own).start()
-
-    @pl.loop(1, n)
-    def _(step):
-        to = lax.rem(me + step, n)
-        pltpu.make_async_remote_copy(
-            src_ref=packed.at[step],
-            dst_ref=out_ref.at[me],
-            send_sem=out_send,
-            recv_sem=out_recv,
-            device_id=(to // lon_n, lax.rem(to, lon_n)),
-            device_id_type=MESH,
-        ).start()
+    for turn in range(lat_n):
+        to_lat = lax.rem(lat + turn, lat_n)
+
+        @pl.loop(0, lon_n)
+        def _(step):
+            base = (to_lat * lon_n + lax.rem(lon + step, lon_n)) * ROWS
+            here = pl.multiple_of((turn * lon_n + step) * ROWS, ROWS)
+            for r in range(ROWS):
+                picked[pl.ds(here + r, 1), :] = fourier[pl.ds(order[base + r], 1), :]
+            packed[turn * lon_n + step] = picked[pl.ds(here, ROWS), :].astype(jnp.bfloat16)
+
+        if turn == 0:
+            pltpu.make_async_copy(packed.at[0], out_ref.at[me], out_own).start()
+
+        @pl.loop(0 if turn else 1, lon_n)
+        def _(step):
+            pltpu.make_async_remote_copy(
+                src_ref=packed.at[turn * lon_n + step],
+                dst_ref=out_ref.at[me],
+                send_sem=out_send,
+                recv_sem=out_recv,
+                device_id=(to_lat, lax.rem(lon + step, lon_n)),
+                device_id_type=MESH,
+            ).start()
 
     for c in range(CHUNKS):
         pltpu.make_async_copy(sent.at[pl.ds(1, lon_n - 1), c], sent.at[pl.ds(1, lon_n - 1), c], send_sem.at[c]).wait()
@@ -192,61 +195,73 @@
 KB = 256
 
 
-def legendre_kernel(limits, moved_ref, table, out, table_in, moved, data, result, table_sem, out_sem):
+def prepare(moved, data, s):
+    lane = lax.broadcasted_iota(jnp.int32, (16, 128), 1) // 32
+    for half in range(2):
+        xs = [moved[pl.ds((half * 4 + i) * 256 + s, 16, stride=ROWS), :] for i in range(4)]
+        for g in range(4):
+            rolled = [x if i == g else pltpu.roll(x, (i - g) % 4 * 32, 1) for i, x in enumerate(xs)]
+            low = jnp.where(lane < 1, rolled[0], rolled[1])
+            high = jnp.where(lane < 3, rolled[2], rolled[3])
+            data[s, pl.ds(g * 16, 16), pl.ds(half * 128, 128)] = jnp.where(lane < 2, low, high).astype(jnp.bfloat16)
+
+
+def legendre_kernel(order, moved_ref, table, out, table_in, moved, data, result, zeros, table_sem, out_sem):
     slots, degrees, lats = table_in.shape
     parts = degrees // KB
+    first = (lax.axis_index("lat") * lax.axis_size("lon") + lax.axis_index("lon")) * slots
+
+    def blocks(s):
+        return (degrees - order[first + s] + KB - 1) // KB
 
     def fetch(s, p):
-        at = pl.ds(pl.multiple_of(p * KB, KB), KB)
-        return pltpu.make_async_copy(table.at[s, at], table_in.at[s, at], table_sem.at[s])
+        rows = pl.ds(0, p * KB)
+        return pltpu.make_async_copy(table.at[s, rows], table_in.at[s, rows], table_sem.at[s])
+
+    zeros[...] = jnp.zeros_like(zeros)
 
     @pl.loop(0, slots)
     def _(s):
-        for p in range(parts):
-
-            @pl.when(p * KB < limits[s])
+        count = blocks(s)
+        for p in range(1, parts + 1):
+
+            @pl.when(count == p)
             def _():
                 fetch(s, p).start()
 
-    @pl.loop(0, 128)
-    def _(source):
-        moved[pl.ds(pl.multiple_of(source * ROWS, ROWS), ROWS), :] = moved_ref[source].astype(jnp.float32)
-
-    lane = lax.broadcasted_iota(jnp.int32, (16, 128), 1) // 32
+    @pl.loop(0, 128 // 8)
+    def _(group):
+        for i in range(8):
+            source = group * 8 + i
+            moved[pl.ds(pl.multiple_of(source * ROWS, ROWS), ROWS), :] = moved_ref[source].astype(jnp.float32)
+
+    prepare(moved, data, 0)
 
     @pl.loop(0, slots)
     def _(s):
-        for half in range(2):
-            xs = [moved[pl.ds((half * 4 + i) * 256 + s, 16, stride=ROWS), :] for i in range(4)]
-            for g in range(4):
-                rolled = [x if i == g else pltpu.roll(x, (i - g) % 4 * 32, 1) for i, x in enumerate(xs)]
-                joined = jnp.where(lane < 2, jnp.where(lane < 1, rolled[0], rolled[1]), jnp.where(lane < 3, rolled[2], rolled[3]))
-                data[s, pl.ds(g * 16, 16), pl.ds(half * 128, 128)] = joined.astype(jnp.bfloat16)
-
-    degree = lax.broadcasted_iota(jnp.int32, (1, KB), 1)
-    parity = (1 - 2 * (degree % 2)).astype(jnp.float32)
-
-    @pl.loop(0, slots)
-    def _(s):
-        for p in range(parts):
-            at = pl.ds(p * KB, KB)
-            needed = p * KB < limits[s]
-
-            @pl.when(needed)
+        count = blocks(s)
+        limit = degrees - order[first + s]
+        for p in range(1, parts + 1):
+
+            @pl.when(count == p)
             def _():
                 fetch(s, p).wait()
-                sums = lax.dot_general(data[s], table_in[s, at, :], NT, preferred_element_type=jnp.float32)
-                keep = degree + p * KB < limits[s]
-                for c in range(2):
-                    both = sums[c * 32 : c * 32 + 16] + parity * sums[c * 32 + 16 : c * 32 + 32]
-                    result[s, c, :, at] = jnp.where(keep, both, 0.0)
-
-            @pl.when(jnp.logical_not(needed))
-            def _():
-                for c in range(2):
-                    result[s, c, :, at] = jnp.zeros((16, KB), jnp.float32)
-
-        pltpu.make_async_copy(result.at[s], out.at[s], out_sem).start()
+                for q in range(p):
+                    at = pl.ds(q * KB, KB)
+                    sums = lax.dot_general(data[s], table_in[s, at, :], NT, preferred_element_type=jnp.float32)
+                    degree = lax.broadcasted_iota(jnp.int32, (1, KB), 1)
+                    parity = (1 - 2 * (degree % 2)).astype(jnp.float32)
+                    for c in range(2):
+                        both = sums[c * 32 : c * 32 + 16] + parity * sums[c * 32 + 16 : c * 32 + 32]
+                        if q == p - 1:
+                            both = jnp.where(degree + q * KB < limit, both, 0.0)
+                        result[s, c, :, at] = both
+                prepare(moved, data, lax.rem(s + 1, slots))
+                used = pl.ds(0, p * KB)
+                pltpu.make_async_copy(result.at[s, :, :, used], out.at[s, :, :, used], out_sem).start()
+                if p < parts:
+                    rest = pl.ds(p * KB, degrees - p * KB)
+                    pltpu.make_async_copy(zeros.at[:, :, rest], out.at[s, :, :, rest], out_sem).start()
 
     pltpu.make_async_copy(result, out, out_sem).wait()
 
@@ -287,8 +302,6 @@
         name="fourier",
     )(wave_order, vorticity, jnp.asarray(basis), jnp.asarray(twiddle))
 
-    first_slot = lax.axis_index(("lat", "lon")) * ROWS
-    limits = MW - lax.dynamic_slice_in_dim(wave_order, first_slot, ROWS)
     slots, degrees, lats = legendre.shape
     return pl.pallas_call(
         legendre_kernel,
@@ -300,11 +313,12 @@
             pltpu.VMEM((MW, 128), f32),
             pltpu.VMEM((slots, 64, lats), bf16),
             pltpu.VMEM((slots, 2, 16, degrees), f32),
+            pltpu.VMEM((2, 16, degrees), f32),
             dma((slots,)),
             dma,
         ],
         name="legendre_sums",
-    )(limits, moved, legendre)
+    )(wave_order, moved, legendre)
 
 
 def solution(mesh):

time: 61.2 us -> 45.8 us (0.75)
  the two profiles are of different devices: /device:TPU:9 before, /device:TPU:1 now
where the time goes in v2:
time: 45.8 us; the launch traced here: 45.4 us
  Pallas kernels  45.3 us (99%)
    pallas_call x1, Pallas kernels, on_device(): pl.pallas_call(functools.partial(fourier_kernel, lat_n, lon_n), out_shape...  37.2 us
    pallas_call x1, Pallas kernels, on_device(): pl.pallas_call(legendre_kernel, out_shape=jax.ShapeDtypeStruct((slots, 2,...  8.13 us

profile of v2, /device:TPU:1, one launch (start us, length us, event | category | flops | bytes accessed | tf_op | source)
XLA Modules:
  0.0 45.4 jit_solution(11687989557060816818)
XLA Ops:
  0.0 37.2 %fourier.1.moved_ref = bf16[128,16,128]{2,1,0:T(8,128)(2,1)} custom-call(s32[2048]{0:T(1024)} %order.3, f32[16,2,32,512]{3,2,1,0:T(8,128)} %v_hbm.1, bf16[512,512]{1,0:T(8,128)(2,1)} %constant.4.clone.basis_hbm, f32[24,512]{1,0:T(8,128)} %constant.5.clone.twiddle), custom_call_target="tpu_custom_call" | custom-call | tf_op jit(solution)/shard_map/fourier/pallas_call | solution.py:278
  37.2 8.1 %legendre_sums.1 = f32[16,2,16,2048]{3,2,1,0:T(8,128)} custom-call(s32[2048]{0:T(1024)} %order.3, bf16[128,16,128]{2,1,0:T(8,128)(2,1)} %fourier.1.moved_ref, bf16[16,2048,256]{2,1,0:T(8,128)(2,1)} %table.1), custom_call_target="tpu_custom_call" | custom-call | tf_op jit(solution)/shard_map/legendre_sums/pallas_call | solution.py:306

commit v3 on v2

--- a/solution.py
+++ b/solution.py
@@ -1,4 +1,5 @@
 import functools
+import itertools
 import math
 
 import jax
@@ -63,6 +64,8 @@
 NT = (((1,), (1,)), ((), ()))
 CHUNKS = 4
 CROWS = CIRCLES // CHUNKS
+HALVES = 2
+ZROWS = 10 * 64
 
 
 def fourier_kernel(
@@ -76,13 +79,20 @@
     basis_copy = pltpu.make_async_copy(basis_hbm, basis, load_sem.at[1])
     basis_copy.start()
 
+    x, core, y, z = lat // 2, lax.rem(lat, 2), lon // 4, lax.rem(lon, 4)
+    ring = (2, 1, 3, 0)
+    xs, ys, zs = ([lax.rem(at + d, 4) for d in range(4)] for at in (x, y, z))
+    cores = [core, 1 - core]
+    hops = lambda *shift: -sum(min(d, 4 - d) for d in shift)
+    plane = sorted([(dy, dz) for dy in ring for dz in ring if dy or dz], key=lambda s: hops(*s))
+    peers = [ys[dy] * 4 + zs[dz] for dy, dz in plane]
+
     barrier = pltpu.get_barrier_semaphore()
-    for step in range(1, lon_n):
-        peer = lax.rem(lon + step, lon_n)
+    for peer in peers:
         pl.semaphore_signal(barrier, inc=1, device_id=(lat, peer), device_id_type=MESH)
-    for step in range(1, lat_n):
-        peer = lax.rem(lat + step, lat_n)
-        pl.semaphore_signal(barrier, inc=1, device_id=(peer, lon), device_id_type=MESH)
+    for dx, dc in itertools.product(ring, (1, 0)):
+        if dx or dc:
+            pl.semaphore_signal(barrier, inc=1, device_id=(xs[dx] * 2 + cores[dc], lon), device_id_type=MESH)
 
     v_copy.wait()
 
@@ -96,98 +106,110 @@
     own.start()
     pl.semaphore_wait(barrier, lon_n - 1 + lat_n - 1)
 
-    def exchange(c, step):
-        peer = lax.rem(lon + step, lon_n)
-        return pltpu.make_async_remote_copy(
-            src_ref=sent.at[peer, c],
-            dst_ref=got.at[lon, c],
-            send_sem=send_sem.at[c],
-            recv_sem=recv_sem.at[c],
-            device_id=(lat, peer),
-            device_id_type=MESH,
-        )
-
     for c in range(CHUNKS):
-
-        @pl.loop(1, lon_n)
-        def _(step):
-            exchange(c, step).start()
+        for peer in peers:
+            pltpu.make_async_remote_copy(
+                src_ref=sent.at[peer, c],
+                dst_ref=got.at[lon, c],
+                send_sem=send_sem.at[c],
+                recv_sem=recv_sem.at[c],
+                device_id=(lat, peer),
+                device_id_type=MESH,
+            ).start()
 
     basis_copy.wait()
     own.wait()
-    for c in range(CHUNKS):
+    me = lat * lon_n + lon
+    lane = lax.broadcasted_iota(jnp.int32, (1, 128), 1)
+    real = lax.rem(lane, 64) < 32
+    sign = jnp.where(real, 1.0, -1.0).astype(jnp.float32)
+    for half in range(HALVES):
+        empty = pl.ds(half * ZROWS + 17 * 32, ZROWS - 17 * 32)
+        z_high[empty, :] = jnp.zeros((ZROWS - 17 * 32, SPAN), jnp.bfloat16)
+        z_low[empty, :] = jnp.zeros((ZROWS - 17 * 32, SPAN), jnp.bfloat16)
+
+    def first_stage(c):
         pltpu.make_async_copy(got.at[pl.ds(1, lon_n - 1), c], got.at[pl.ds(1, lon_n - 1), c], recv_sem.at[c]).wait()
+        half, part_of_half = divmod(c, CHUNKS // HALVES)
 
         @pl.loop(0, SPAN // 128)
         def _(part):
             lanes = pl.ds(pl.multiple_of(part * 128, 128), 128)
             blocks = [got[b, c, :, lanes].astype(jnp.float32) for b in range(BLOCKS)]
             for k, (yr, yi) in enumerate(real_dft(blocks)):
-                row = k * 2 * CIRCLES + c * CROWS
+                row = half * ZROWS + k * 64 + part_of_half * CROWS
                 if k == BLOCKS // 2:
-                    zr, zi = yr, None
+                    zs = [yr]
                 else:
                     tc, ts = twiddle[k : k + 1, lanes], twiddle[k + 9 : k + 10, lanes]
                     if yi is None:
-                        zr, zi = yr * tc, yr * ts
+                        zs = [yr * tc, yr * ts]
                     else:
-                        zr, zi = yr * tc - yi * ts, yr * ts + yi * tc
-                high, low = split(zr)
-                z_high[pl.ds(row, CROWS), lanes] = high
-                z_low[pl.ds(row, CROWS), lanes] = low
-                row += CIRCLES
-                if zi is None:
-                    high = low = jnp.zeros((CROWS, 128), jnp.bfloat16)
+                        zs = [yr * tc - yi * ts, yr * ts + yi * tc]
+                for i, z_part in enumerate(zs):
+                    high, low = split(z_part)
+                    z_high[pl.ds(row + i * 32, CROWS), lanes] = high
+                    z_low[pl.ds(row + i * 32, CROWS), lanes] = low
+
+    def second_stage(half):
+        for k0, count in ((0, 4), (4, 4), (8, 2)):
+            rows = pl.ds(half * ZROWS + k0 * 64, count * 64)
+            by_high = lax.dot_general(basis[...], z_high[rows, :], NT, preferred_element_type=jnp.float32)
+            by_low = lax.dot_general(basis[: 2 * HALF, :], z_low[rows, :], NT, preferred_element_type=jnp.float32)
+            both = by_high[: 2 * HALF] + by_high[2 * HALF :] + by_low
+            for pair in range(count // 2):
+                at = slice(pair * 128, pair * 128 + 128)
+                cos_part, sin_part = both[:HALF, at], both[HALF:, at]
+                swapped = jnp.where(real, pltpu.roll(sin_part, 96, 1), pltpu.roll(sin_part, 32, 1))
+                plus, minus = cos_part + sign * swapped, sign * cos_part - swapped
+                k = k0 + pair * 2
+                for value, first, second in ((plus, k, k + 1), (minus, BLOCKS - k, BLOCKS - k - 1)):
+                    turned = pltpu.roll(value, 64, 1)
+                    for wave, row in ((first, jnp.where(lane < 64, value, turned)), (second, jnp.where(lane < 64, turned, value))):
+                        if (wave <= BLOCKS // 2) if value is plus else (BLOCKS // 2 < wave < BLOCKS):
+                            fourier[pl.ds(wave, HALF, stride=BLOCKS), :] = row
+
+    def send_slots(half):
+        for group, (dx, dy) in enumerate(itertools.product(ring, ring)):
+
+            @pl.loop(0, 2)
+            def _(t):
+                for u in range(4):
+                    to_z, to_core = lax.rem(z + t * 2 + u // 2, 4), cores[u % 2]
+                    base = ((xs[dx] * 2 + to_core) * lon_n + ys[dy] * 4 + to_z) * ROWS
+                    here = pl.multiple_of((group * 8 + t * 4 + u) * ROWS, ROWS)
+                    for r in range(ROWS):
+                        picked[pl.ds(here + r, 1), :] = fourier[pl.ds(order[base + r], 1), :]
+                for u in range(4):
+                    here = pl.multiple_of((group * 8 + t * 4 + u) * ROWS, ROWS)
+                    pair = jnp.where(lane < 64, picked[pl.ds(here, 8), :], picked[pl.ds(here + 8, 8), :])
+                    packed[half, group * 8 + t * 4 + u] = pair.astype(jnp.bfloat16)
+
+            for dz, dc in itertools.product(ring, (1, 0)):
+                message = packed.at[half, group * 8 + dz * 2 + dc]
+                if dx or dy or dz or dc:
+                    pltpu.make_async_remote_copy(
+                        src_ref=message,
+                        dst_ref=out_ref.at[half, me],
+                        send_sem=out_send,
+                        recv_sem=out_recv,
+                        device_id=(xs[dx] * 2 + cores[dc], ys[dy] * 4 + zs[dz]),
+                        device_id_type=MESH,
+                    ).start()
                 else:
-                    high, low = split(zi)
-                z_high[pl.ds(row, CROWS), lanes] = high
-                z_low[pl.ds(row, CROWS), lanes] = low
-
-    lane = lax.broadcasted_iota(jnp.int32, (1, 128), 1)
-    sign = jnp.where(lane < CIRCLES, 1.0, -1.0).astype(jnp.float32)
-    for k in range(BLOCKS // 2 + 1):
-        rows = pl.ds(k * 128, 128)
-        by_high = lax.dot_general(basis[...], z_high[rows, :], NT, preferred_element_type=jnp.float32)
-        by_low = lax.dot_general(basis[: 2 * HALF, :], z_low[rows, :], NT, preferred_element_type=jnp.float32)
-        both = by_high[: 2 * HALF] + by_high[2 * HALF :] + by_low
-        cos_part = both[:HALF]
-        sin_part = pltpu.roll(both[HALF:], CIRCLES, 1)
-        fourier[pl.ds(k, HALF, stride=BLOCKS), :] = cos_part + sign * sin_part
-        if 0 < k < BLOCKS // 2:
-            fourier[pl.ds(BLOCKS - k, HALF, stride=BLOCKS), :] = sign * cos_part - sin_part
-
-    me = lat * lon_n + lon
-    n = lat_n * lon_n
-
-    for turn in range(lat_n):
-        to_lat = lax.rem(lat + turn, lat_n)
-
-        @pl.loop(0, lon_n)
-        def _(step):
-            base = (to_lat * lon_n + lax.rem(lon + step, lon_n)) * ROWS
-            here = pl.multiple_of((turn * lon_n + step) * ROWS, ROWS)
-            for r in range(ROWS):
-                picked[pl.ds(here + r, 1), :] = fourier[pl.ds(order[base + r], 1), :]
-            packed[turn * lon_n + step] = picked[pl.ds(here, ROWS), :].astype(jnp.bfloat16)
-
-        if turn == 0:
-            pltpu.make_async_copy(packed.at[0], out_ref.at[me], out_own).start()
-
-        @pl.loop(0 if turn else 1, lon_n)
-        def _(step):
-            pltpu.make_async_remote_copy(
-                src_ref=packed.at[turn * lon_n + step],
-                dst_ref=out_ref.at[me],
-                send_sem=out_send,
-                recv_sem=out_recv,
-                device_id=(to_lat, lax.rem(lon + step, lon_n)),
-                device_id_type=MESH,
-            ).start()
+                    pltpu.make_async_copy(message, out_ref.at[half, me], out_own.at[half]).start()
+
+    for half in range(HALVES):
+        for c in range(half * CHUNKS // HALVES, (half + 1) * CHUNKS // HALVES):
+            first_stage(c)
+        second_stage(half)
+        send_slots(half)
 
     for c in range(CHUNKS):
         pltpu.make_async_copy(sent.at[pl.ds(1, lon_n - 1), c], sent.at[pl.ds(1, lon_n - 1), c], send_sem.at[c]).wait()
-    pltpu.make_async_copy(packed.at[0], out_ref.at[me], out_own).wait()
-    rest = packed.at[pl.ds(1, n - 1)]
+    for half in range(HALVES):
+        pltpu.make_async_copy(packed.at[half, 0], out_ref.at[half, me], out_own.at[half]).wait()
+    rest = packed.at[:, pl.ds(0, lat_n * lon_n - 1)]
     pltpu.make_async_copy(rest, rest, out_send).wait()
     pltpu.make_async_copy(rest, rest, out_recv).wait()
 
@@ -195,15 +217,16 @@
 KB = 256
 
 
-def prepare(moved, data, s):
+def prepare(moved, data, r, half):
     lane = lax.broadcasted_iota(jnp.int32, (16, 128), 1) // 32
-    for half in range(2):
-        xs = [moved[pl.ds((half * 4 + i) * 256 + s, 16, stride=ROWS), :] for i in range(4)]
+    for k in range(2):
+        xs = [moved[pl.ds(half * 1024 + (k * 4 + i) * 128 + r, 16, stride=8), :] for i in range(4)]
         for g in range(4):
             rolled = [x if i == g else pltpu.roll(x, (i - g) % 4 * 32, 1) for i, x in enumerate(xs)]
             low = jnp.where(lane < 1, rolled[0], rolled[1])
             high = jnp.where(lane < 3, rolled[2], rolled[3])
-            data[s, pl.ds(g * 16, 16), pl.ds(half * 128, 128)] = jnp.where(lane < 2, low, high).astype(jnp.bfloat16)
+            rows = pl.ds(pl.multiple_of((g % 2 * 2 + half) * 16, 16), 16)
+            data[g // 2 * 8 + r, rows, pl.ds(k * 128, 128)] = jnp.where(lane < 2, low, high).astype(jnp.bfloat16)
 
 
 def legendre_kernel(order, moved_ref, table, out, table_in, moved, data, result, zeros, table_sem, out_sem):
@@ -221,7 +244,8 @@
     zeros[...] = jnp.zeros_like(zeros)
 
     @pl.loop(0, slots)
-    def _(s):
+    def _(t):
+        s = lax.rem(t, 2) * 8 + t // 2
         count = blocks(s)
         for p in range(1, parts + 1):
 
@@ -229,16 +253,21 @@
             def _():
                 fetch(s, p).start()
 
-    @pl.loop(0, 128 // 8)
-    def _(group):
-        for i in range(8):
-            source = group * 8 + i
-            moved[pl.ds(pl.multiple_of(source * ROWS, ROWS), ROWS), :] = moved_ref[source].astype(jnp.float32)
-
-    prepare(moved, data, 0)
+    for half in range(HALVES):
+
+        @pl.loop(0, 128 // 16)
+        def _(group):
+            for i in range(16):
+                source = group * 16 + i
+                row = pl.multiple_of(half * 1024 + source * 8, 8)
+                moved[pl.ds(row, 8), :] = moved_ref[half, source].astype(jnp.float32)
+
+        prepare(moved, data, 0, half)
 
     @pl.loop(0, slots)
-    def _(s):
+    def _(t):
+        half, pair = lax.rem(t, 2), t // 2
+        s = half * 8 + pair
         count = blocks(s)
         limit = degrees - order[first + s]
         for p in range(1, parts + 1):
@@ -256,7 +285,7 @@
                         if q == p - 1:
                             both = jnp.where(degree + q * KB < limit, both, 0.0)
                         result[s, c, :, at] = both
-                prepare(moved, data, lax.rem(s + 1, slots))
+                prepare(moved, data, lax.rem(pair + 1, 8), half)
                 used = pl.ds(0, p * KB)
                 pltpu.make_async_copy(result.at[s, :, :, used], out.at[s, :, :, used], out_sem).start()
                 if p < parts:
@@ -277,7 +306,7 @@
     dma = pltpu.SemaphoreType.DMA
     moved = pl.pallas_call(
         functools.partial(fourier_kernel, lat_n, lon_n),
-        out_shape=jax.ShapeDtypeStruct((n, ROWS, 128), bf16),
+        out_shape=jax.ShapeDtypeStruct((HALVES, n, ROWS // 2, 128), bf16),
         in_specs=[smem, hbm, hbm, vmem],
         out_specs=hbm,
         scratch_shapes=[
@@ -285,18 +314,18 @@
             pltpu.VMEM(basis.shape, bf16),
             pltpu.VMEM((lon_n, CHUNKS, CROWS, SPAN), bf16),
             pltpu.VMEM((lon_n, CHUNKS, CROWS, SPAN), bf16),
-            pltpu.VMEM((9 * 128, SPAN), bf16),
-            pltpu.VMEM((9 * 128, SPAN), bf16),
+            pltpu.VMEM((HALVES * ZROWS, SPAN), bf16),
+            pltpu.VMEM((HALVES * ZROWS, SPAN), bf16),
             pltpu.VMEM((MW, 128), f32),
             pltpu.VMEM((MW, 128), f32),
-            pltpu.VMEM((n, ROWS, 128), bf16),
+            pltpu.VMEM((HALVES, n, ROWS // 2, 128), bf16),
             dma((2,)),
             dma((CHUNKS,)),
             dma((CHUNKS,)),
             dma,
             dma,
             dma,
-            dma,
+            dma((HALVES,)),
         ],
         compiler_params=pltpu.CompilerParams(collective_id=0, has_side_effects=True),
         name="fourier",

time: 45.8 us -> 42.3 us (0.924)
  Pallas kernels: 45.3 us -> 41.6 us
    pallas_call x1, Pallas kernels: 37.2 us -> 33.5 us  [on_device(): pl.pallas_call(functools.partial(fourier_kernel, lat_n, lon_n), out_shape...]
where the time goes in v3:
time: 42.3 us; the launch traced here: 41.6 us
  Pallas kernels  41.6 us (98%)
    pallas_call x1, Pallas kernels, on_device(): pl.pallas_call(functools.partial(fourier_kernel, lat_n, lon_n), out_shape...  33.5 us
    pallas_call x1, Pallas kernels, on_device(): pl.pallas_call(legendre_kernel, out_shape=jax.ShapeDtypeStruct((slots, 2,...  8.1 us

profile of v3, /device:TPU:1, one launch (start us, length us, event | category | flops | bytes accessed | tf_op | source)
XLA Modules:
  0.0 41.6 jit_solution(3892635715586338975)
XLA Ops:
  0.0 33.5 %fourier.1.moved_ref = bf16[2,128,8,128]{3,2,1,0:T(8,128)(2,1)} custom-call(s32[2048]{0:T(1024)} %order.3, f32[16,2,32,512]{3,2,1,0:T(8,128)} %v_hbm.1, bf16[512,512]{1,0:T(8,128)(2,1)} %constant.4.clone.basis_hbm, f32[24,512]{1,0:T(8,128)} %constant.5.clone.twiddle), custom_call_target="tpu_custom_call" | custom-call | tf_op jit(solution)/shard_map/fourier/pallas_call | solution.py:307
  33.5 8.1 %legendre_sums.1 = f32[16,2,16,2048]{3,2,1,0:T(8,128)} custom-call(s32[2048]{0:T(1024)} %order.3, bf16[2,128,8,128]{3,2,1,0:T(8,128)(2,1)} %fourier.1.moved_ref, bf16[16,2048,256]{2,1,0:T(8,128)(2,1)} %table.1), custom_call_target="tpu_custom_call" | custom-call | tf_op jit(solution)/shard_map/legendre_sums/pallas_call | solution.py:335

commit v4 on v3

--- a/solution.py
+++ b/solution.py
@@ -65,11 +65,12 @@
 CHUNKS = 4
 CROWS = CIRCLES // CHUNKS
 HALVES = 2
+GRANT = 49_737_728
 ZROWS = 10 * 64
 
 
 def fourier_kernel(
-    lat_n, lon_n, order, v_hbm, basis_hbm, twiddle, out_ref,
+    lat_n, lon_n, order, v_hbm, basis_hbm, twiddle, table_hbm, out_ref, table_ref,
     v_in, basis, sent, got, z_high, z_low, fourier, picked, packed,
     load_sem, send_sem, recv_sem, own_sem, out_send, out_recv, out_own,
 ):
@@ -95,6 +96,8 @@
             pl.semaphore_signal(barrier, inc=1, device_id=(xs[dx] * 2 + cores[dc], lon), device_id_type=MESH)
 
     v_copy.wait()
+    table_copy = pltpu.make_async_copy(table_hbm, table_ref, load_sem.at[2])
+    table_copy.start()
 
     @pl.loop(0, lon_n)
     def _(level):
@@ -169,41 +172,52 @@
                         if (wave <= BLOCKS // 2) if value is plus else (BLOCKS // 2 < wave < BLOCKS):
                             fourier[pl.ds(wave, HALF, stride=BLOCKS), :] = row
 
-    def send_slots(half):
-        for group, (dx, dy) in enumerate(itertools.product(ring, ring)):
-
-            @pl.loop(0, 2)
-            def _(t):
-                for u in range(4):
-                    to_z, to_core = lax.rem(z + t * 2 + u // 2, 4), cores[u % 2]
-                    base = ((xs[dx] * 2 + to_core) * lon_n + ys[dy] * 4 + to_z) * ROWS
-                    here = pl.multiple_of((group * 8 + t * 4 + u) * ROWS, ROWS)
-                    for r in range(ROWS):
-                        picked[pl.ds(here + r, 1), :] = fourier[pl.ds(order[base + r], 1), :]
-                for u in range(4):
-                    here = pl.multiple_of((group * 8 + t * 4 + u) * ROWS, ROWS)
-                    pair = jnp.where(lane < 64, picked[pl.ds(here, 8), :], picked[pl.ds(here + 8, 8), :])
-                    packed[half, group * 8 + t * 4 + u] = pair.astype(jnp.bfloat16)
-
-            for dz, dc in itertools.product(ring, (1, 0)):
-                message = packed.at[half, group * 8 + dz * 2 + dc]
-                if dx or dy or dz or dc:
-                    pltpu.make_async_remote_copy(
-                        src_ref=message,
-                        dst_ref=out_ref.at[half, me],
-                        send_sem=out_send,
-                        recv_sem=out_recv,
-                        device_id=(xs[dx] * 2 + cores[dc], ys[dy] * 4 + zs[dz]),
-                        device_id_type=MESH,
-                    ).start()
-                else:
-                    pltpu.make_async_copy(message, out_ref.at[half, me], out_own.at[half]).start()
-
-    for half in range(HALVES):
-        for c in range(half * CHUNKS // HALVES, (half + 1) * CHUNKS // HALVES):
-            first_stage(c)
-        second_stage(half)
-        send_slots(half)
+    def gather(half, group):
+        dx, dy = groups[group]
+
+        @pl.loop(0, 2)
+        def _(t):
+            for u in range(4):
+                to_z, to_core = lax.rem(z + t * 2 + u // 2, 4), cores[u % 2]
+                base = ((xs[dx] * 2 + to_core) * lon_n + ys[dy] * 4 + to_z) * ROWS
+                here = pl.multiple_of((group * 8 + t * 4 + u) * ROWS, ROWS)
+                for r in range(ROWS):
+                    picked[pl.ds(here + r, 1), :] = fourier[pl.ds(order[base + r], 1), :]
+            for u in range(4):
+                here = pl.multiple_of((group * 8 + t * 4 + u) * ROWS, ROWS)
+                pair = jnp.where(lane < 64, picked[pl.ds(here, 8), :], picked[pl.ds(here + 8, 8), :])
+                packed[half, group * 8 + t * 4 + u] = pair.astype(jnp.bfloat16)
+
+    def send(half, group):
+        dx, dy = groups[group]
+        for dz, dc in itertools.product(ring, (1, 0)):
+            message = packed.at[half, group * 8 + dz * 2 + dc]
+            if dx or dy or dz or dc:
+                pltpu.make_async_remote_copy(
+                    src_ref=message,
+                    dst_ref=out_ref.at[half, me],
+                    send_sem=out_send,
+                    recv_sem=out_recv,
+                    device_id=(xs[dx] * 2 + cores[dc], ys[dy] * 4 + zs[dz]),
+                    device_id_type=MESH,
+                ).start()
+            else:
+                pltpu.make_async_copy(message, out_ref.at[half, me], out_own.at[half]).start()
+
+    groups = list(itertools.product(ring, ring))
+    first_stage(0)
+    first_stage(1)
+    second_stage(0)
+    for g in range(16):
+        gather(0, g)
+    first_stage(2)
+    for g in range(16):
+        send(0, g)
+    first_stage(3)
+    second_stage(1)
+    for g in range(16):
+        gather(1, g)
+        send(1, g)
 
     for c in range(CHUNKS):
         pltpu.make_async_copy(sent.at[pl.ds(1, lon_n - 1), c], sent.at[pl.ds(1, lon_n - 1), c], send_sem.at[c]).wait()
@@ -212,6 +226,7 @@
     rest = packed.at[:, pl.ds(0, lat_n * lon_n - 1)]
     pltpu.make_async_copy(rest, rest, out_send).wait()
     pltpu.make_async_copy(rest, rest, out_recv).wait()
+    table_copy.wait()
 
 
 KB = 256
@@ -229,7 +244,7 @@
             data[g // 2 * 8 + r, rows, pl.ds(k * 128, 128)] = jnp.where(lane < 2, low, high).astype(jnp.bfloat16)
 
 
-def legendre_kernel(order, moved_ref, table, out, table_in, moved, data, result, zeros, table_sem, out_sem):
+def legendre_kernel(order_hbm, moved_ref, table_in, out, order, moved, data, result, zeros, order_sem, out_sem):
     slots, degrees, lats = table_in.shape
     parts = degrees // KB
     first = (lax.axis_index("lat") * lax.axis_size("lon") + lax.axis_index("lon")) * slots
@@ -237,21 +252,9 @@
     def blocks(s):
         return (degrees - order[first + s] + KB - 1) // KB
 
-    def fetch(s, p):
-        rows = pl.ds(0, p * KB)
-        return pltpu.make_async_copy(table.at[s, rows], table_in.at[s, rows], table_sem.at[s])
-
+    order_copy = pltpu.make_async_copy(order_hbm, order, order_sem)
+    order_copy.start()
     zeros[...] = jnp.zeros_like(zeros)
-
-    @pl.loop(0, slots)
-    def _(t):
-        s = lax.rem(t, 2) * 8 + t // 2
-        count = blocks(s)
-        for p in range(1, parts + 1):
-
-            @pl.when(count == p)
-            def _():
-                fetch(s, p).start()
 
     for half in range(HALVES):
 
@@ -263,6 +266,8 @@
                 moved[pl.ds(row, 8), :] = moved_ref[half, source].astype(jnp.float32)
 
         prepare(moved, data, 0, half)
+
+    order_copy.wait()
 
     @pl.loop(0, slots)
     def _(t):
@@ -274,7 +279,6 @@
 
             @pl.when(count == p)
             def _():
-                fetch(s, p).wait()
                 for q in range(p):
                     at = pl.ds(q * KB, KB)
                     sums = lax.dot_general(data[s], table_in[s, at, :], NT, preferred_element_type=jnp.float32)
@@ -304,11 +308,11 @@
     vmem = pl.BlockSpec(memory_space=pltpu.VMEM)
     smem = pl.BlockSpec(memory_space=pltpu.SMEM)
     dma = pltpu.SemaphoreType.DMA
-    moved = pl.pallas_call(
+    moved, table = pl.pallas_call(
         functools.partial(fourier_kernel, lat_n, lon_n),
-        out_shape=jax.ShapeDtypeStruct((HALVES, n, ROWS // 2, 128), bf16),
-        in_specs=[smem, hbm, hbm, vmem],
-        out_specs=hbm,
+        out_shape=(pltpu.VMEM((HALVES, n, ROWS // 2, 128), bf16), pltpu.VMEM(legendre.shape, bf16)),
+        in_specs=[smem, hbm, hbm, vmem, hbm],
+        out_specs=(vmem, vmem),
         scratch_shapes=[
             pltpu.VMEM(vorticity.shape, f32),
             pltpu.VMEM(basis.shape, bf16),
@@ -319,7 +323,7 @@
             pltpu.VMEM((MW, 128), f32),
             pltpu.VMEM((MW, 128), f32),
             pltpu.VMEM((HALVES, n, ROWS // 2, 128), bf16),
-            dma((2,)),
+            dma((3,)),
             dma((CHUNKS,)),
             dma((CHUNKS,)),
             dma,
@@ -327,27 +331,30 @@
             dma,
             dma((HALVES,)),
         ],
-        compiler_params=pltpu.CompilerParams(collective_id=0, has_side_effects=True),
+        compiler_params=pltpu.CompilerParams(collective_id=0, has_side_effects=True, vmem_limit_bytes=GRANT),
         name="fourier",
-    )(wave_order, vorticity, jnp.asarray(basis), jnp.asarray(twiddle))
+    )(wave_order, vorticity, jnp.asarray(basis), jnp.asarray(twiddle), legendre)
 
     slots, degrees, lats = legendre.shape
+    moved = pltpu.with_memory_space_constraint(moved, pltpu.VMEM)
+    table = pltpu.with_memory_space_constraint(table, pltpu.VMEM)
     return pl.pallas_call(
         legendre_kernel,
         out_shape=jax.ShapeDtypeStruct((slots, 2, 16, degrees), f32),
-        in_specs=[smem, vmem, hbm],
+        in_specs=[hbm, vmem, vmem],
         out_specs=hbm,
         scratch_shapes=[
-            pltpu.VMEM(legendre.shape, bf16),
+            pltpu.SMEM(wave_order.shape, jnp.int32),
             pltpu.VMEM((MW, 128), f32),
             pltpu.VMEM((slots, 64, lats), bf16),
             pltpu.VMEM((slots, 2, 16, degrees), f32),
             pltpu.VMEM((2, 16, degrees), f32),
-            dma((slots,)),
+            dma,
             dma,
         ],
+        compiler_params=pltpu.CompilerParams(vmem_limit_bytes=GRANT),
         name="legendre_sums",
-    )(wave_order, moved, legendre)
+    )(wave_order, moved, table)
 
 
 def solution(mesh):

time: 42.3 us -> 40 us (0.946); the launches traced: 41.6 us -> 39.9 us
  Pallas kernels: 41.6 us -> 39.9 us
    pallas_call x1, Pallas kernels: 8.1 us -> 7.2 us  [on_device(): pl.pallas_call(legendre_kernel, out_shape=jax.ShapeDtypeStruct((slots, 2,...]
    pallas_call x1, Pallas kernels: 33.5 us -> 32.7 us  [on_device(): pl.pallas_call(functools.partial(fourier_kernel, lat_n, lon_n), out_shape...]
where the time goes in v4:
time: 40 us; the launch traced here: 39.9 us
  Pallas kernels  39.9 us (100%)
    pallas_call x1, Pallas kernels, on_device(): pl.pallas_call(functools.partial(fourier_kernel, lat_n, lon_n), out_shape...  32.7 us
    pallas_call x1, Pallas kernels, on_device(): pl.pallas_call(legendre_kernel, out_shape=jax.ShapeDtypeStruct((slots, 2,...  7.2 us

profile of v4, /device:TPU:1, one launch (start us, length us, event | category | flops | bytes accessed | tf_op | source)
XLA Modules:
  0.0 39.9 jit_solution(12209662963567030502)
XLA Ops:
  0.0 32.7 %fourier.1 = (bf16[2,128,8,128]{3,2,1,0:T(8,128)(2,1)S(1)}, bf16[16,2048,256]{2,1,0:T(8,128)(2,1)S(1)}) custom-call(s32[2048]{0:T(1024)} %order_hbm.1, f32[16,2,32,512]{3,2,1,0:T(8,128)} %v_hbm.1, bf16[512,512]{1,0:T(8,128)(2,1)} %constant.4.clone.basis_hbm, f32[24,512]{1,0:T(8,128)} %constant.5.clone.twiddle, bf16[16,2048,256]{2,1,0:T(8,128)(2,1)} %table_hbm.1), custom_call_target="tpu_custom_call" | custom-call | tf_op jit(solution)/shard_map/fourier/pallas_call | solution.py:311
  32.7 7.2 %legendre_sums.1 = f32[16,2,16,2048]{3,2,1,0:T(8,128)} custom-call(s32[2048]{0:T(1024)} %order_hbm.1, bf16[2,128,8,128]{3,2,1,0:T(8,128)(2,1)S(1)} %get-tuple-element.7.moved_ref, bf16[16,2048,256]{2,1,0:T(8,128)(2,1)S(1)} %get-tuple-element.8.table_in), custom_call_target="tpu_custom_call" | custom-call | tf_op jit(solution)/shard_map/legendre_sums/pallas_call | solution.py:341

commit v5 on v4

--- a/solution.py
+++ b/solution.py
@@ -70,16 +70,11 @@
 
 
 def fourier_kernel(
-    lat_n, lon_n, order, v_hbm, basis_hbm, twiddle, table_hbm, out_ref, table_ref,
-    v_in, basis, sent, got, z_high, z_low, fourier, picked, packed,
+    lat_n, lon_n, order_hbm, v_hbm, basis_hbm, twiddle_hbm, table_hbm, out_ref, table_ref,
+    order, v_in, basis, twiddle, sent, got, z_high, z_low, fourier, picked, packed,
     load_sem, send_sem, recv_sem, own_sem, out_send, out_recv, out_own,
 ):
     lat, lon = lax.axis_index("lat"), lax.axis_index("lon")
-    v_copy = pltpu.make_async_copy(v_hbm, v_in, load_sem.at[0])
-    v_copy.start()
-    basis_copy = pltpu.make_async_copy(basis_hbm, basis, load_sem.at[1])
-    basis_copy.start()
-
     x, core, y, z = lat // 2, lax.rem(lat, 2), lon // 4, lax.rem(lon, 4)
     ring = (2, 1, 3, 0)
     xs, ys, zs = ([lax.rem(at + d, 4) for d in range(4)] for at in (x, y, z))
@@ -95,6 +90,15 @@
         if dx or dc:
             pl.semaphore_signal(barrier, inc=1, device_id=(xs[dx] * 2 + cores[dc], lon), device_id_type=MESH)
 
+    v_copy = pltpu.make_async_copy(v_hbm, v_in, load_sem.at[0])
+    v_copy.start()
+    basis_copy = pltpu.make_async_copy(basis_hbm, basis, load_sem.at[1])
+    basis_copy.start()
+    order_copy = pltpu.make_async_copy(order_hbm, order, load_sem.at[3])
+    order_copy.start()
+    twiddle_copy = pltpu.make_async_copy(twiddle_hbm, twiddle, load_sem.at[4])
+    twiddle_copy.start()
+
     v_copy.wait()
     table_copy = pltpu.make_async_copy(table_hbm, table_ref, load_sem.at[2])
     table_copy.start()
@@ -114,13 +118,15 @@
             pltpu.make_async_remote_copy(
                 src_ref=sent.at[peer, c],
                 dst_ref=got.at[lon, c],
-                send_sem=send_sem.at[c],
+                send_sem=send_sem,
                 recv_sem=recv_sem.at[c],
                 device_id=(lat, peer),
                 device_id_type=MESH,
             ).start()
 
     basis_copy.wait()
+    order_copy.wait()
+    twiddle_copy.wait()
     own.wait()
     me = lat * lon_n + lon
     lane = lax.broadcasted_iota(jnp.int32, (1, 128), 1)
@@ -205,22 +211,23 @@
                 pltpu.make_async_copy(message, out_ref.at[half, me], out_own.at[half]).start()
 
     groups = list(itertools.product(ring, ring))
-    first_stage(0)
-    first_stage(1)
+    for c in range(CHUNKS // 2):
+        first_stage(c)
     second_stage(0)
     for g in range(16):
         gather(0, g)
-    first_stage(2)
+    for c in range(CHUNKS // 2, CHUNKS - 1):
+        first_stage(c)
     for g in range(16):
         send(0, g)
-    first_stage(3)
+    first_stage(CHUNKS - 1)
     second_stage(1)
     for g in range(16):
         gather(1, g)
         send(1, g)
 
-    for c in range(CHUNKS):
-        pltpu.make_async_copy(sent.at[pl.ds(1, lon_n - 1), c], sent.at[pl.ds(1, lon_n - 1), c], send_sem.at[c]).wait()
+    blocks = sent.at[pl.ds(1, lon_n - 1)]
+    pltpu.make_async_copy(blocks, blocks, send_sem).wait()
     for half in range(HALVES):
         pltpu.make_async_copy(packed.at[half, 0], out_ref.at[half, me], out_own.at[half]).wait()
     rest = packed.at[:, pl.ds(0, lat_n * lon_n - 1)]
@@ -306,16 +313,17 @@
     bf16, f32 = jnp.bfloat16, jnp.float32
     hbm = pl.BlockSpec(memory_space=pl.ANY)
     vmem = pl.BlockSpec(memory_space=pltpu.VMEM)
-    smem = pl.BlockSpec(memory_space=pltpu.SMEM)
     dma = pltpu.SemaphoreType.DMA
     moved, table = pl.pallas_call(
         functools.partial(fourier_kernel, lat_n, lon_n),
         out_shape=(pltpu.VMEM((HALVES, n, ROWS // 2, 128), bf16), pltpu.VMEM(legendre.shape, bf16)),
-        in_specs=[smem, hbm, hbm, vmem, hbm],
+        in_specs=[hbm, hbm, hbm, hbm, hbm],
         out_specs=(vmem, vmem),
         scratch_shapes=[
+            pltpu.SMEM(wave_order.shape, jnp.int32),
             pltpu.VMEM(vorticity.shape, f32),
             pltpu.VMEM(basis.shape, bf16),
+            pltpu.VMEM(twiddle.shape, f32),
             pltpu.VMEM((lon_n, CHUNKS, CROWS, SPAN), bf16),
             pltpu.VMEM((lon_n, CHUNKS, CROWS, SPAN), bf16),
             pltpu.VMEM((HALVES * ZROWS, SPAN), bf16),
@@ -323,8 +331,8 @@
             pltpu.VMEM((MW, 128), f32),
             pltpu.VMEM((MW, 128), f32),
             pltpu.VMEM((HALVES, n, ROWS // 2, 128), bf16),
-            dma((3,)),
-            dma((CHUNKS,)),
+            dma((5,)),
+            dma,
             dma((CHUNKS,)),
             dma,
             dma,

time: 40 us -> 38.7 us (0.968); the launches traced: 39.9 us -> 38.1 us
  Pallas kernels: 39.9 us -> 38.1 us
    pallas_call x1, Pallas kernels: 7.2 us -> 6.28 us  [on_device(): pl.pallas_call(legendre_kernel, out_shape=jax.ShapeDtypeStruct((slots, 2,...]
    pallas_call x1, Pallas kernels: 32.7 us -> 31.8 us  [on_device(): pl.pallas_call(functools.partial(fourier_kernel, lat_n, lon_n), out_shape...]
where the time goes in v5:
time: 38.7 us; the launch traced here: 38.1 us
  Pallas kernels  38.1 us (98%)
    pallas_call x1, Pallas kernels, on_device(): pl.pallas_call(functools.partial(fourier_kernel, lat_n, lon_n), out_shape...  31.8 us
    pallas_call x1, Pallas kernels, on_device(): pl.pallas_call(legendre_kernel, out_shape=jax.ShapeDtypeStruct((slots, 2,...  6.28 us

profile of v5, /device:TPU:1, one launch (start us, length us, event | category | flops | bytes accessed | tf_op | source)
XLA Modules:
  0.0 38.1 jit_solution(12172541089278451394)
XLA Ops:
  0.0 31.8 %fourier.1 = (bf16[2,128,8,128]{3,2,1,0:T(8,128)(2,1)S(1)}, bf16[16,2048,256]{2,1,0:T(8,128)(2,1)S(1)}) custom-call(s32[2048]{0:T(1024)} %order_hbm.3, f32[16,2,32,512]{3,2,1,0:T(8,128)} %v_hbm.1, bf16[512,512]{1,0:T(8,128)(2,1)} %constant.4.clone.basis_hbm, f32[24,512]{1,0:T(8,128)} %constant.5.clone.twiddle_hbm, bf16[16,2048,256]{2,1,0:T(8,128)(2,1)} %table_hbm.1), custom_call_target="tpu_custom_call" | custom-call | tf_op jit(solution)/shard_map/fourier/pallas_call | solution.py:317
  31.8 6.3 %legendre_sums.1 = f32[16,2,16,2048]{3,2,1,0:T(8,128)} custom-call(s32[2048]{0:T(1024)} %order_hbm.3, bf16[2,128,8,128]{3,2,1,0:T(8,128)(2,1)S(1)} %get-tuple-element.7.moved_ref, bf16[16,2048,256]{2,1,0:T(8,128)(2,1)S(1)} %get-tuple-element.8.table_in), custom_call_target="tpu_custom_call" | custom-call | tf_op jit(solution)/shard_map/legendre_sums/pallas_call | solution.py:349

commit v6 on v5

--- a/solution.py
+++ b/solution.py
@@ -210,7 +210,7 @@
             else:
                 pltpu.make_async_copy(message, out_ref.at[half, me], out_own.at[half]).start()
 
-    groups = list(itertools.product(ring, ring))
+    groups = sorted(itertools.product(ring, ring), key=lambda s: hops(*s))
     for c in range(CHUNKS // 2):
         first_stage(c)
     second_stage(0)

time: 38.7 us -> 39 us (level); the launches traced: 38.1 us -> 38.8 us
  Pallas kernels: 38.1 us -> 38.8 us
    pallas_call x1, Pallas kernels: 6.28 us -> 7.22 us  [on_device(): pl.pallas_call(legendre_kernel, out_shape=jax.ShapeDtypeStruct((slots, 2,...]
where the time goes in v6:
time: 39 us; the launch traced here: 38.8 us
  Pallas kernels  38.8 us (99%)
    pallas_call x1, Pallas kernels, on_device(): pl.pallas_call(functools.partial(fourier_kernel, lat_n, lon_n), out_shape...  31.6 us
    pallas_call x1, Pallas kernels, on_device(): pl.pallas_call(legendre_kernel, out_shape=jax.ShapeDtypeStruct((slots, 2,...  7.22 us

profile of v6, /device:TPU:1, one launch (start us, length us, event | category | flops | bytes accessed | tf_op | source)
XLA Modules:
  0.0 38.8 jit_solution(4933297125984815460)
XLA Ops:
  0.0 31.6 %fourier.1 = (bf16[2,128,8,128]{3,2,1,0:T(8,128)(2,1)S(1)}, bf16[16,2048,256]{2,1,0:T(8,128)(2,1)S(1)}) custom-call(s32[2048]{0:T(1024)} %order_hbm.3, f32[16,2,32,512]{3,2,1,0:T(8,128)} %v_hbm.1, bf16[512,512]{1,0:T(8,128)(2,1)} %constant.4.clone.basis_hbm, f32[24,512]{1,0:T(8,128)} %constant.5.clone.twiddle_hbm, bf16[16,2048,256]{2,1,0:T(8,128)(2,1)} %table_hbm.1), custom_call_target="tpu_custom_call" | custom-call | tf_op jit(solution)/shard_map/fourier/pallas_call | solution.py:317
  31.6 7.2 %legendre_sums.1 = f32[16,2,16,2048]{3,2,1,0:T(8,128)} custom-call(s32[2048]{0:T(1024)} %order_hbm.3, bf16[2,128,8,128]{3,2,1,0:T(8,128)(2,1)S(1)} %get-tuple-element.7.moved_ref, bf16[16,2048,256]{2,1,0:T(8,128)(2,1)S(1)} %get-tuple-element.8.table_in), custom_call_target="tpu_custom_call" | custom-call | tf_op jit(solution)/shard_map/legendre_sums/pallas_call | solution.py:349
